TPU v7x, 32 devices: a whole 2x2x4 slice. The times are simulated.
32 devices in a mesh: groups: 2 (over x), ctx: 8 (over z, y), head: 2 (over core).
Axes of the slice: x: 2, y: 2, z: 4, core: 2. Of those that a mesh axis runs over, the one named last changes fastest.
Arguments:
- queries: bfloat16 [4096, 4, 8, 128], P(('groups', 'ctx'), 'head'), parts along dimension 0, may hold values from -40 to 40
- keys: bfloat16 [4096, 4, 128], P(('groups', 'ctx'), 'head'), parts along dimension 0, may hold values from -6 to 6
- values: bfloat16 [4096, 4, 128], P(('groups', 'ctx'), 'head'), parts along dimension 0, may hold values from -6 to 6
- segments: int32 [4096], P(('groups', 'ctx')), parts along dimension 0, may hold values from 0 to 3, never falling along the last dimension, each value on 1 to 1024 neighbouring positions
- score_weight: bfloat16 [4, 8, 128], P('head'), may hold values from -0.09375 to 0.09375
Outputs:
- attended: bfloat16 [4096, 4, 8, 128], P(('groups', 'ctx'), 'head'), parts along dimension 0
- score: float32 [4096], P(('groups', 'ctx')), parts along dimension 0
There are 2 independent parts, one for each index of `groups`. A program takes and returns all parts, laid end to end along the dimension named above; an argument that names none is the same for every part. Nothing has to cross between parts.
Inputs may be any that keep to these rules, and one draw needn't show every extreme that they name: `segments`: document ids never fall along the sequence; each document covers 1 to 1024 positions and one covers exactly 1024.
All inputs are finite; a program needn't handle non-finite values.
Results may differ from a plain program's by a relative error of at most 0.0032.
Values may be sent and summed in bfloat16 or wider, within the bound.
A program may use at most 64 MiB of HBM per device.

v0:
```python
import functools
import math

import jax
import jax.numpy as jnp
from jax import lax
from jax.experimental import pallas as pl
from jax.experimental.pallas import tpu as pltpu
from jax.sharding import PartitionSpec as P

MESH = pl.DeviceIdType.MESH
F32 = jnp.float32
BF16 = jnp.bfloat16
PAD = 16
TILE = 512
HIDE = -1e30


def kernel(n, window, q_ref, kv_ref, sw_ref, out_ref, score_ref,
           slots, qs, kx, held, acc, mstat, vt, swt, spread, prow, part, part_in,
           lane_send, cross_send, recv, score_sem):
    heads, rows, group, hd = q_ref.shape[1], q_ref.shape[0], q_ref.shape[2], q_ref.shape[3]
    flat = rows * group
    half = window // 2
    c = lax.axis_index("ctx")
    hc = lax.axis_index("head")
    is_odd = lax.rem(c, 2)
    partner = c + 1 - 2 * is_odd
    factor = math.log2(math.e) / math.sqrt(hd)
    spread_rows = spread.shape[0]
    tile_pos = TILE // group

    barrier = pltpu.get_barrier_semaphore()
    has_next = c + 2 < n
    has_prev = c >= 2

    @pl.when(has_next)
    def _():
        pl.semaphore_signal(barrier, inc=1, device_id={"ctx": c + 2}, device_id_type=MESH)

    @pl.when(has_prev)
    def _():
        pl.semaphore_signal(barrier, inc=1, device_id={"ctx": c - 2}, device_id_type=MESH)

    pl.semaphore_signal(barrier, inc=1, device_id={"ctx": partner}, device_id_type=MESH)
    pl.semaphore_signal(barrier, inc=1, device_id={"head": 1 - hc}, device_id_type=MESH)

    def block_of(d, h):
        return kv_ref.at[h] if d == 0 else slots.at[d - 1, h]

    def lane_copy(k, h):
        return pltpu.make_async_remote_copy(
            src_ref=block_of(2 * k, h), dst_ref=slots.at[2 * k + 1, h],
            send_sem=lane_send.at[k, h], recv_sem=recv.at[2 * k + 1, h],
            device_id={"ctx": c + 2}, device_id_type=MESH)

    def cross_even(k, h):
        return pltpu.make_async_remote_copy(
            src_ref=block_of(2 * k, h), dst_ref=slots.at[2 * k, h],
            send_sem=cross_send.at[k, h], recv_sem=recv.at[2 * k, h],
            device_id={"ctx": partner}, device_id_type=MESH)

    def cross_odd(k, h):
        return pltpu.make_async_remote_copy(
            src_ref=block_of(2 * k, h), dst_ref=slots.at[2 * k - 2, h],
            send_sem=cross_send.at[k, h], recv_sem=recv.at[2 * k - 2, h],
            device_id={"ctx": partner}, device_id_type=MESH)

    def sends(k, h, act):
        held = c >= 2 * k
        if k < half:
            @pl.when(held & has_next)
            def _():
                act(lane_copy(k, h))

            @pl.when(held & (is_odd == 0))
            def _():
                act(cross_even(k, h))
        if k >= 1:
            @pl.when(held & (is_odd == 1))
            def _():
                act(cross_odd(k, h))

    def wait_block(d, h):
        pltpu.make_async_remote_copy(
            src_ref=slots.at[d - 1, h], dst_ref=slots.at[d - 1, h],
            send_sem=lane_send.at[0, h], recv_sem=recv.at[d - 1, h],
            device_id={"ctx": partner}, device_id_type=MESH).wait_recv()

    pl.semaphore_wait(barrier, 2 + has_next.astype(jnp.int32) + has_prev.astype(jnp.int32))
    for h in range(heads):
        sends(0, h, lambda copy: copy.start())

    lane_id = lax.broadcasted_iota(jnp.int32, (rows, hd), 1).astype(F32)

    def ids_by_row(block):
        ids = block[rows:rows + PAD, :].astype(F32)[0:1, :]
        return jnp.broadcast_to(ids, (hd, rows)).T

    hidden = jnp.where(ids_by_row(kv_ref.at[0]) == lane_id, 0.0, HIDE)
    hidden = jnp.broadcast_to(hidden[:, None, :], (rows, group, hd)).reshape(flat, hd).astype(BF16)
    for h in range(heads):
        qs[h, :, 0:hd] = q_ref[:, h].astype(F32).reshape(flat, hd).astype(BF16)
        qs[h, :, hd:] = hidden
        vt[h, hd:, :] = jnp.ones((vt.shape[1] - hd, rows), BF16)
        one = sw_ref[h].astype(F32)
        many = jnp.broadcast_to(one[None], (TILE // group, group, hd)).reshape(TILE, hd)
        swt[h] = many.T
    spread[...] = (
        lax.broadcasted_iota(jnp.int32, spread.shape, 0) // group
        == lax.broadcasted_iota(jnp.int32, spread.shape, 1)
    ).astype(F32)

    def attend(d, h):
        block = block_of(d, h)
        if h == 0:
            match = jnp.where(ids_by_row(block) == lane_id, 1.0, 0.0).astype(BF16)
            for other in range(heads):
                kx[other, :, hd:] = match
        kx[h, :, 0:hd] = block[0:rows, 0:hd]
        vt[h, 0:hd, :] = block[0:rows, hd:2 * hd].astype(F32).T.astype(BF16)

        def extent(t):
            low, high = 0, rows
            if d == 0:
                high = min(rows, (t + 1) * tile_pos)
            elif d == window:
                low = t * tile_pos // 16 * 16
            return low, high

        def scores(t):
            low, high = extent(t)
            got = lax.dot_general(kx[h, low:high, :], qs[h, t * TILE:(t + 1) * TILE, :],
                                  (((1,), (1,)), ((), ())), preferred_element_type=F32)
            if d == 0:
                key_pos = lax.broadcasted_iota(jnp.int32, (high - low, TILE), 0)
                query_pos = (t * TILE + lax.broadcasted_iota(jnp.int32, (1, TILE), 1)) // group
                got = jnp.where(key_pos <= query_pos, got, HIDE)
            held[t % 4, low:high, :] = got
            return jnp.max(got, axis=0, keepdims=True)

        def tile(t, top):
            low, high = extent(t)
            cols = slice(t * TILE, (t + 1) * TILE)
            if d > 0:
                old = mstat[h, 0:1, cols]
                top = jnp.maximum(old, top)
            p = jnp.exp2((held[t % 4, low:high, :] - top) * factor).astype(BF16)
            first, last = low // 128 * 128, -(-high // 128) * 128
            parts = [p]
            if low > first:
                parts = [jnp.zeros((low - first, TILE), BF16)] + parts
            if last > high:
                parts = parts + [jnp.zeros((last - high, TILE), BF16)]
            p = jnp.concatenate(parts, axis=0) if len(parts) > 1 else p
            new = jnp.dot(vt[h, :, first:last], p, preferred_element_type=F32)
            if d > 0:
                new = new + acc[h, :, cols] * jnp.exp2((old - top) * factor)
            acc[h, :, cols] = new
            mstat[h, :, cols] = jnp.broadcast_to(top, (8, TILE))

        tiles = flat // TILE
        ready = [scores(t) for t in range(min(3, tiles))]
        for t in range(tiles):
            if t + 3 < tiles:
                ready.append(scores(t + 3))
            tile(t, ready[t])

    for h in range(heads):
        attend(0, h)
    def take_and_forward(k, h):
        @pl.when(c >= 2 * k)
        def _():
            wait_block(2 * k, h)
            sends(k, h, lambda copy: copy.start())

    for h in range(heads):
        take_and_forward(1, h)
    for k in range(1, half + 1):
        @pl.when(c >= 2 * k)
        def _():
            for h in range(heads):
                attend(2 * k, h)

        for h in range(heads):
            if k < half:
                take_and_forward(k + 1, h)

            @pl.when(c >= 2 * k - 1)
            def _():
                wait_block(2 * k - 1, h)
                attend(2 * k - 1, h)

    def finish(i, carry):
        start = pl.multiple_of(i * TILE, TILE)
        cols = pl.ds(start, TILE)
        line = jnp.zeros((1, TILE), F32)
        for h in range(heads):
            got = acc[h, 0:hd, cols] / acc[h, hd:hd + 1, cols]
            got = got.astype(BF16).astype(F32)
            line = line + jnp.sum(got * swt[h], axis=0, keepdims=True)
            out_ref[pl.ds(i * tile_pos, tile_pos), h] = got.T.reshape(tile_pos, group, hd).astype(BF16)
        prow[:, cols] = jnp.broadcast_to(line, (8, TILE))
        return carry

    lax.fori_loop(0, flat // TILE, finish, 0)
    for piece in range(flat // spread_rows):
        part[:, piece * 128:(piece + 1) * 128] = jnp.dot(
            prow[:, piece * spread_rows:(piece + 1) * spread_rows], spread[...],
            precision=lax.Precision.HIGHEST, preferred_element_type=F32)
    share = pltpu.make_async_remote_copy(
        src_ref=part, dst_ref=part_in, send_sem=score_sem.at[0], recv_sem=score_sem.at[1],
        device_id={"head": 1 - hc}, device_id_type=MESH)
    share.start()
    for k in range(half + 1):
        for h in range(heads):
            sends(k, h, lambda copy: copy.wait_send())
    share.wait()
    score_ref[...] = (part[...] + part_in[...])[0:1, :]


def local(n, queries, keys, values, segments, score_weight):
    rows, heads, group, hd = queries.shape
    window = max(2, n // 2)
    flat = rows * group
    head_blocks = jnp.concatenate([keys, values], axis=-1).transpose(1, 0, 2)
    ids = jnp.broadcast_to(segments.astype(BF16)[None, None, :], (heads, PAD, rows))
    kv = jnp.concatenate([head_blocks, ids], axis=1)
    vmem = pl.BlockSpec(memory_space=pltpu.VMEM)
    attended, score = pl.pallas_call(
        functools.partial(kernel, n, window),
        out_shape=(
            pltpu.VMEM(queries.shape, BF16),
            jax.ShapeDtypeStruct((1, rows), F32),
        ),
        in_specs=[vmem] * 3,
        out_specs=(vmem, vmem),
        scratch_shapes=[
            pltpu.VMEM((window, heads, rows + PAD, 2 * hd), BF16),
            pltpu.VMEM((heads, flat, 2 * hd), BF16),
            pltpu.VMEM((heads, rows, 2 * hd), BF16),
            pltpu.VMEM((4, rows, TILE), F32),
            pltpu.VMEM((heads, hd + PAD, flat), F32),
            pltpu.VMEM((heads, 8, flat), F32),
            pltpu.VMEM((heads, hd + PAD, rows), BF16),
            pltpu.VMEM((heads, hd, TILE), F32),
            pltpu.VMEM((128 * group, 128), F32),
            pltpu.VMEM((8, flat), F32),
            pltpu.VMEM((8, rows), F32),
            pltpu.VMEM((8, rows), F32),
            pltpu.SemaphoreType.DMA((window // 2 + 1, heads)),
            pltpu.SemaphoreType.DMA((window // 2 + 1, heads)),
            pltpu.SemaphoreType.DMA((window, heads)),
            pltpu.SemaphoreType.DMA((2,)),
        ],
        compiler_params=pltpu.CompilerParams(collective_id=0, has_side_effects=True),
    )(queries, kv, score_weight)
    return attended, score.reshape(rows)


def solution(mesh):
    return jax.shard_map(
        functools.partial(local, mesh.shape["ctx"]),
        mesh=mesh,
        in_specs=(
            P(("groups", "ctx"), "head", None, None),
            P(("groups", "ctx"), "head", None),
            P(("groups", "ctx"), "head", None),
            P(("groups", "ctx")),
            P("head", None, None),
        ),
        out_specs=(P(("groups", "ctx"), "head", None, None), P(("groups", "ctx"))),
        check_vma=False,
    )
```

profile of v0, /device:TPU:17, one launch (start us, length us, event | category | flops | bytes accessed | tf_op | source)
XLA Modules:
  0.0 30.8 jit_solution(5569724697616168642)
XLA Ops:
  0.6 0.7 %convert_element_type.3 = bf16[256]{0:T(256)(128)(2,1)S(1)} convert(s32[256]{0:T(256)} %param.8) | non-fusion elementwise | flops 256 | bytes 1536 | tf_op jit(solution)/shard_map/convert_element_type | solution.py:227
  1.3 0.0 copy-start
  1.3 1.0 %copy.7 = bf16[256,2,128]{2,0,1:T(8,128)(2,1)S(1)} copy(bf16[256,2,128]{2,1,0:T(2,128)(2,1)} %param.6) | data formatting | bytes 262144 | tf_op args[1]
  2.3 0.0 copy-done
  2.4 0.7 %pad_maximum_fusion.kv_ref = bf16[2,272,256]{2,1,0:T(8,128)(2,1)} fusion(bf16[2,16,256]{2,1,0:T(8,128)(2,1)S(1)} %broadcast_in_dim.2, bf16[2,256,256]{2,1,0:T(8,128)(2,1)S(1)} %maximum_bitcast_fusion), kind=kLoop, calls=%fused_computation | loop fusion | flops 557056 | bytes 557056 | tf_op jit(solution)/shard_map/concatenate | solution.py:228
  3.1 25.5 %shard_map.68 = (bf16[256,2,8,128]{3,2,1,0:T(8,128)(2,1)S(1)}, f32[1,256]{1,0:T(1,128)}) custom-call(bf16[256,2,8,128]{3,2,1,0:T(8,128)(2,1)} %q_ref.1, bf16[2,272,256]{2,1,0:T(8,128)(2,1)} %pad_maximum_fusion.kv_ref, bf16[2,8,128]{2,1,0:T(8,128)(2,1)} %sw_ref.1), custom_call_target="tpu_custom_call" | custom-call | tf_op jit(solution)/shard_map/pallas_call | solution.py:230
  28.6 1.0 %copy.11 = bf16[256,2,8,128]{3,2,1,0:T(8,128)(2,1)} copy(bf16[256,2,8,128]{3,2,1,0:T(8,128)(2,1)S(1)} %get-tuple-element.6) | data formatting | bytes 2097152
  29.6 0.0 copy-start.1
  29.6 0.7 %copy-done.1 = f32[1,256]{1,0:T(1,128)S(1)} copy-done((f32[1,256]{1,0:T(1,128)S(1)}, f32[1,256]{1,0:T(1,128)}, u32[]{:S(2)}) %copy-start.1) | copy-done | bytes 1048
  30.3 0.6 %copy.12 = f32[256]{0:T(256)} copy(f32[256]{0:T(256)S(1)} %bitcast.3) | data formatting | bytes 2048
  (3 shorter events, 0.1 us)
Async XLA Ops:
  1.3 1.0 %copy-start = (bf16[256,2,128]{2,1,0:T(2,128)(2,1)S(1)}, bf16[256,2,128]{2,1,0:T(2,128)(2,1)}, u32[]{:S(2)}) copy-start(bf16[256,2,128]{2,1,0:T(2,128)(2,1)} %param.7) | copy-start | bytes 393220
  29.6 0.7 %copy-start.1 = (f32[1,256]{1,0:T(1,128)S(1)}, f32[1,256]{1,0:T(1,128)}, u32[]{:S(2)}) copy-start(f32[1,256]{1,0:T(1,128)} %get-tuple-element.5) | copy-start | bytes 3076
where the time goes:
time: 31 us; the launch traced here: 30.8 us
  Pallas kernels  25.5 us (82%)
  local copies, waits for them, and re-layouts  3.19 us (10%)
  other arithmetic  1.44 us (5%)
  between operations  0.66 us (2%)
    pallas_call x1, Pallas kernels, local(): pl.pallas_call(functools.partial(kernel, n, window), out_shape=(pltpu.VME...  25.5 us
    unnamed x8, local copies, waits for them, and re-layouts  3.19 us
    concatenate x1, other arithmetic, local(): kv = jnp.concatenate([head_blocks, ids], axis=1)  0.73 us
    convert_element_type x1, other arithmetic, local(): segments.astype(BF16)[None, None, :]  0.68 us

commit v1 on v0

v1 whole, which is shorter than its diff:
```python
import functools
import math

import jax
import jax.numpy as jnp
from jax import lax
from jax.experimental import pallas as pl
from jax.experimental.pallas import tpu as pltpu
from jax.sharding import PartitionSpec as P

MESH = pl.DeviceIdType.MESH
F32 = jnp.float32
BF16 = jnp.bfloat16
PAD = 16
TILE = 512
HIDE = -1e30
PARTS = 2


def kernel(n, window, q_hbm, k_hbm, v_hbm, ids_hbm, sw_hbm, out_ref, score_ref,
           ks, vs, ids, qv, swv, wide, qs, kx, held, acc, mstat, vt, swt, spread, prow, part, part_in,
           load_sem, lane_send, cross_send, recv, score_sem):
    rows, heads, group, hd = q_hbm.shape
    flat = rows * group
    half = window // 2
    c = lax.axis_index("ctx")
    hc = lax.axis_index("head")
    is_odd = lax.rem(c, 2)
    partner = c + 1 - 2 * is_odd
    factor = math.log2(math.e) / math.sqrt(hd)
    spread_rows = spread.shape[0]
    tile_pos = TILE // group
    cut = rows * heads // PARTS
    chunks = 1 + 2 * PARTS

    barrier = pltpu.get_barrier_semaphore()
    has_next = c + 2 < n
    has_prev = c >= 2

    @pl.when(has_next)
    def _():
        pl.semaphore_signal(barrier, inc=1, device_id={"ctx": c + 2}, device_id_type=MESH)

    @pl.when(has_prev)
    def _():
        pl.semaphore_signal(barrier, inc=1, device_id={"ctx": c - 2}, device_id_type=MESH)

    pl.semaphore_signal(barrier, inc=1, device_id={"ctx": partner}, device_id_type=MESH)
    pl.semaphore_signal(barrier, inc=1, device_id={"head": 1 - hc}, device_id_type=MESH)

    loads = [
        pltpu.make_async_copy(src, dst, load_sem.at[i])
        for i, (src, dst) in enumerate((
            (q_hbm, qv), (ids_hbm, ids.at[0]), (k_hbm, ks.at[0]), (v_hbm, vs.at[0]), (sw_hbm, swv)))
    ]
    for load in loads:
        load.start()

    def piece(d, j, own):
        if j == 0:
            return ids_hbm if own else ids.at[d]
        which, at = divmod(j - 1, PARTS)
        span = pl.ds(at * cut, cut)
        if own:
            return (k_hbm, v_hbm)[which].at[span, :]
        return (ks, vs)[which].at[d, span, :]

    def lane_copy(k, j):
        return pltpu.make_async_remote_copy(
            src_ref=piece(2 * k, j, k == 0), dst_ref=piece(2 * k + 2, j, False),
            send_sem=lane_send.at[k, j], recv_sem=recv.at[2 * k + 1, j],
            device_id={"ctx": c + 2}, device_id_type=MESH)

    def cross_even(k, j):
        return pltpu.make_async_remote_copy(
            src_ref=piece(2 * k, j, k == 0), dst_ref=piece(2 * k + 1, j, False),
            send_sem=cross_send.at[k, j], recv_sem=recv.at[2 * k, j],
            device_id={"ctx": partner}, device_id_type=MESH)

    def cross_odd(k, j):
        return pltpu.make_async_remote_copy(
            src_ref=piece(2 * k, j, k == 0), dst_ref=piece(2 * k - 1, j, False),
            send_sem=cross_send.at[k, j], recv_sem=recv.at[2 * k - 2, j],
            device_id={"ctx": partner}, device_id_type=MESH)

    def sends(k, j, act):
        held_here = c >= 2 * k
        if k < half:
            @pl.when(held_here & has_next)
            def _():
                act(lane_copy(k, j))

            @pl.when(held_here & (is_odd == 0))
            def _():
                act(cross_even(k, j))
        if k >= 1:
            @pl.when(held_here & (is_odd == 1))
            def _():
                act(cross_odd(k, j))

    def wait_piece(d, j):
        pltpu.make_async_remote_copy(
            src_ref=piece(d, j, False), dst_ref=piece(d, j, False),
            send_sem=lane_send.at[0, j], recv_sem=recv.at[d - 1, j],
            device_id={"ctx": partner}, device_id_type=MESH).wait_recv()

    def forward(k, j):
        sending = c >= 2 * k
        if k == half:
            sending = sending & (is_odd == 1)

        @pl.when(sending)
        def _():
            wait_piece(2 * k, j)
            sends(k, j, lambda copy: copy.start())

    pl.semaphore_wait(barrier, 2 + has_next.astype(jnp.int32) + has_prev.astype(jnp.int32))
    for j in range(chunks):
        sends(0, j, lambda copy: copy.start())

    lane_id = lax.broadcasted_iota(jnp.int32, (rows, hd), 1).astype(F32)

    def ids_by_row(d):
        return jnp.broadcast_to(ids[d].astype(F32), (hd, rows)).T

    def split_heads(block):
        wide[...] = block[...].astype(F32)
        return [wide[pl.ds(h, rows, stride=heads), :] for h in range(heads)]

    loads[4].wait()
    for h in range(heads):
        vt[h, hd:, :] = jnp.ones((vt.shape[1] - hd, rows), BF16)
        one = swv[h].astype(F32)
        many = jnp.broadcast_to(one[None], (TILE // group, group, hd)).reshape(TILE, hd)
        swt[h] = many.T
    spread[...] = (
        lax.broadcasted_iota(jnp.int32, spread.shape, 0) // group
        == lax.broadcasted_iota(jnp.int32, spread.shape, 1)
    ).astype(F32)
    loads[1].wait()
    hidden = jnp.where(ids_by_row(0) == lane_id, 0.0, HIDE)
    hidden = jnp.broadcast_to(hidden[:, None, :], (rows, group, hd)).reshape(flat, hd).astype(BF16)
    loads[0].wait()
    for h in range(heads):
        qs[h, :, 0:hd] = qv[:, h].astype(F32).reshape(flat, hd).astype(BF16)
        qs[h, :, hd:] = hidden

    def prepare(d):
        match = jnp.where(ids_by_row(d) == lane_id, 1.0, 0.0).astype(BF16)
        for h, key in enumerate(split_heads(ks.at[d])):
            kx[h, :, 0:hd] = key.astype(BF16)
            kx[h, :, hd:] = match
        for h, value in enumerate(split_heads(vs.at[d])):
            vt[h, 0:hd, :] = value.T.astype(BF16)

    def attend(d, h):
        def extent(t):
            low, high = 0, rows
            if d == 0:
                high = min(rows, (t + 1) * tile_pos)
            elif d == window:
                low = t * tile_pos // 16 * 16
            return low, high

        def scores(t):
            low, high = extent(t)
            got = lax.dot_general(kx[h, low:high, :], qs[h, t * TILE:(t + 1) * TILE, :],
                                  (((1,), (1,)), ((), ())), preferred_element_type=F32)
            if d == 0:
                key_pos = lax.broadcasted_iota(jnp.int32, (high - low, TILE), 0)
                query_pos = (t * TILE + lax.broadcasted_iota(jnp.int32, (1, TILE), 1)) // group
                got = jnp.where(key_pos <= query_pos, got, HIDE)
            held[t % 4, low:high, :] = got
            return jnp.max(got, axis=0, keepdims=True)

        def tile(t, top):
            low, high = extent(t)
            cols = slice(t * TILE, (t + 1) * TILE)
            if d > 0:
                old = mstat[h, 0:1, cols]
                top = jnp.maximum(old, top)
            p = jnp.exp2((held[t % 4, low:high, :] - top) * factor).astype(BF16)
            first, last = low // 128 * 128, -(-high // 128) * 128
            parts = [p]
            if low > first:
                parts = [jnp.zeros((low - first, TILE), BF16)] + parts
            if last > high:
                parts = parts + [jnp.zeros((last - high, TILE), BF16)]
            p = jnp.concatenate(parts, axis=0) if len(parts) > 1 else p
            new = jnp.dot(vt[h, :, first:last], p, preferred_element_type=F32)
            if d > 0:
                new = new + acc[h, :, cols] * jnp.exp2((old - top) * factor)
            acc[h, :, cols] = new
            mstat[h, :, cols] = jnp.broadcast_to(top, (8, TILE))

        tiles = flat // TILE
        ready = [scores(t) for t in range(min(3, tiles))]
        for t in range(tiles):
            if t + 3 < tiles:
                ready.append(scores(t + 3))
            tile(t, ready[t])

    def wait_rest(d):
        if d % 2 == 0 and d // 2 < half:
            return
        for j in range(chunks):
            if d % 2 == 0:
                @pl.when(is_odd == 0)
                def _():
                    wait_piece(d, j)
            else:
                wait_piece(d, j)

    def at_each_forward(k):
        plan = [[0, 1]] + [[j] for j in range(2, chunks)]
        for some in plan:
            if k <= half:
                for j in some:
                    forward(k, j)
            yield

    points = at_each_forward(1)
    loads[2].wait()
    loads[3].wait()
    prepare(0)
    for h in range(heads):
        attend(0, h)
        next(points, None)
    for _ in points:
        pass
    for k in range(1, half + 1):
        points = at_each_forward(k + 1)
        for d in (2 * k, 2 * k - 1):
            @pl.when(c >= d)
            def _():
                wait_rest(d)
                prepare(d)

            for h in range(heads):
                @pl.when(c >= d)
                def _():
                    attend(d, h)
                next(points, None)
        for _ in points:
            pass

    def finish(i, carry):
        start = pl.multiple_of(i * TILE, TILE)
        cols = pl.ds(start, TILE)
        line = jnp.zeros((1, TILE), F32)
        for h in range(heads):
            got = acc[h, 0:hd, cols] * (1.0 / acc[h, hd:hd + 1, cols])
            got = got.astype(BF16).astype(F32)
            line = line + jnp.sum(got * swt[h], axis=0, keepdims=True)
            out_ref[pl.ds(i * tile_pos, tile_pos), h] = got.T.reshape(tile_pos, group, hd).astype(BF16)
        prow[:, cols] = jnp.broadcast_to(line, (8, TILE))
        return carry

    lax.fori_loop(0, flat // TILE, finish, 0)
    for at in range(flat // spread_rows):
        part[:, at * 128:(at + 1) * 128] = jnp.dot(
            prow[:, at * spread_rows:(at + 1) * spread_rows], spread[...],
            precision=lax.Precision.HIGHEST, preferred_element_type=F32)
    share = pltpu.make_async_remote_copy(
        src_ref=part, dst_ref=part_in, send_sem=score_sem.at[0], recv_sem=score_sem.at[1],
        device_id={"head": 1 - hc}, device_id_type=MESH)
    share.start()
    for k in range(half + 1):
        for j in range(chunks):
            sends(k, j, lambda copy: copy.wait_send())
    share.wait()
    score_ref[...] = (part[...] + part_in[...])[0:1, :]


def local(n, queries, keys, values, segments, score_weight):
    rows, heads, group, hd = queries.shape
    window = max(2, n // 2)
    flat = rows * group
    chunks = 1 + 2 * PARTS
    anywhere = pl.BlockSpec(memory_space=pl.ANY)
    vmem = pl.BlockSpec(memory_space=pltpu.VMEM)
    attended, score = pl.pallas_call(
        functools.partial(kernel, n, window),
        out_shape=(
            pltpu.VMEM(queries.shape, BF16),
            jax.ShapeDtypeStruct((1, rows), F32),
        ),
        in_specs=[anywhere] * 5,
        out_specs=(vmem, vmem),
        scratch_shapes=[
            pltpu.VMEM((window + 1, rows * heads, hd), BF16),
            pltpu.VMEM((window + 1, rows * heads, hd), BF16),
            pltpu.VMEM((window + 1, 1, rows), jnp.int32),
            pltpu.VMEM(queries.shape, BF16),
            pltpu.VMEM(score_weight.shape, BF16),
            pltpu.VMEM((rows * heads, hd), F32),
            pltpu.VMEM((heads, flat, 2 * hd), BF16),
            pltpu.VMEM((heads, rows, 2 * hd), BF16),
            pltpu.VMEM((4, rows, TILE), F32),
            pltpu.VMEM((heads, hd + PAD, flat), F32),
            pltpu.VMEM((heads, 8, flat), F32),
            pltpu.VMEM((heads, hd + PAD, rows), BF16),
            pltpu.VMEM((heads, hd, TILE), F32),
            pltpu.VMEM((128 * group, 128), F32),
            pltpu.VMEM((8, flat), F32),
            pltpu.VMEM((8, rows), F32),
            pltpu.VMEM((8, rows), F32),
            pltpu.SemaphoreType.DMA((5,)),
            pltpu.SemaphoreType.DMA((window // 2, chunks)),
            pltpu.SemaphoreType.DMA((window // 2 + 1, chunks)),
            pltpu.SemaphoreType.DMA((window, chunks)),
            pltpu.SemaphoreType.DMA((2,)),
        ],
        compiler_params=pltpu.CompilerParams(collective_id=0, has_side_effects=True),
    )(queries, keys.reshape(rows * heads, hd), values.reshape(rows * heads, hd), segments.reshape(1, rows), score_weight)
    return attended, score.reshape(rows)


def solution(mesh):
    return jax.shard_map(
        functools.partial(local, mesh.shape["ctx"]),
        mesh=mesh,
        in_specs=(
            P(("groups", "ctx"), "head", None, None),
            P(("groups", "ctx"), "head", None),
            P(("groups", "ctx"), "head", None),
            P(("groups", "ctx")),
            P("head", None, None),
        ),
        out_specs=(P(("groups", "ctx"), "head", None, None), P(("groups", "ctx"))),
        check_vma=False,
    )
```

time: 31 us -> 26.3 us (0.85)
  Pallas kernels: 25.5 us -> 23.3 us
  other arithmetic: 1.44 us -> 0 us
  local copies, waits for them, and re-layouts: 3.19 us -> 2.19 us
    pallas_call x1, Pallas kernels: 25.5 us -> 23.3 us  [local(): pl.pallas_call(functools.partial(kernel, n, window), out_shape=(pltpu.VME...]
    unnamed x8 -> x4, local copies, waits for them, and re-layouts: 3.19 us -> 2.19 us
    concatenate x1 -> x0, other arithmetic: 0.73 us -> none  [local(): kv = jnp.concatenate([head_blocks, ids], axis=1)]
    convert_element_type x1 -> x0, other arithmetic: 0.68 us -> none  [local(): segments.astype(BF16)[None, None, :]]
where the time goes in v1:
time: 26.3 us; the launch traced here: 26.2 us
  Pallas kernels  23.3 us (89%)
  local copies, waits for them, and re-layouts  2.19 us (8%)
  between operations  0.64 us (2%)
    pallas_call x1, Pallas kernels, local(): pl.pallas_call(functools.partial(kernel, n, window), out_shape=(pltpu.VME...  23.3 us
    unnamed x4, local copies, waits for them, and re-layouts  2.19 us

profile of v1, /device:TPU:17, one launch (start us, length us, event | category | flops | bytes accessed | tf_op | source)
XLA Modules:
  0.0 26.2 jit_solution(4238642744775283405)
XLA Ops:
  0.6 23.3 %shard_map.68 = (bf16[256,2,8,128]{3,2,1,0:T(8,128)(2,1)S(1)}, f32[1,256]{1,0:T(1,128)}) custom-call(bf16[256,2,8,128]{3,2,1,0:T(8,128)(2,1)} %q_hbm.1, bf16[512,128]{1,0:T(8,128)(2,1)} %bitcast.4, bf16[512,128]{1,0:T(8,128)(2,1)} %bitcast.5, s32[1,256]{1,0:T(1,128)} %bitcast.7, bf16[2,8,128]{2,1,0:T(8,128)(2,1)} %sw_hbm.1), custom_call_target="tpu_custom_call" | custom-call | tf_op jit(solution)/shard_map/pallas_call | solution.py:282
  24.0 1.0 %copy.9 = bf16[256,2,8,128]{3,2,1,0:T(8,128)(2,1)} copy(bf16[256,2,8,128]{3,2,1,0:T(8,128)(2,1)S(1)} %get-tuple-element.6) | data formatting | bytes 2097152
  24.9 0.0 copy-start
  24.9 0.7 %copy-done = f32[1,256]{1,0:T(1,128)S(1)} copy-done((f32[1,256]{1,0:T(1,128)S(1)}, f32[1,256]{1,0:T(1,128)}, u32[]{:S(2)}) %copy-start) | copy-done | bytes 1048
  25.6 0.6 %copy.10 = f32[256]{0:T(256)} copy(f32[256]{0:T(256)S(1)} %bitcast.6) | data formatting | bytes 2048
Async XLA Ops:
  24.9 0.7 %copy-start = (f32[1,256]{1,0:T(1,128)S(1)}, f32[1,256]{1,0:T(1,128)}, u32[]{:S(2)}) copy-start(f32[1,256]{1,0:T(1,128)} %get-tuple-element.5) | copy-start | bytes 3076

commit v2 on v1

--- a/solution.py
+++ b/solution.py
@@ -15,10 +15,11 @@
 TILE = 512
 HIDE = -1e30
 PARTS = 2
+OUTS = 4
 
 
 def kernel(n, window, q_hbm, k_hbm, v_hbm, ids_hbm, sw_hbm, out_ref, score_ref,
-           ks, vs, ids, qv, swv, wide, qs, kx, held, acc, mstat, vt, swt, spread, prow, part, part_in,
+           ks, vs, ids, qv, swv, wide, qs, kx, held, acc, mstat, vt, swt, spread, later, shrink, done, part, part_in,
            load_sem, lane_send, cross_send, recv, score_sem):
     rows, heads, group, hd = q_hbm.shape
     flat = rows * group
@@ -136,7 +137,7 @@
     spread[...] = (
         lax.broadcasted_iota(jnp.int32, spread.shape, 0) // group
         == lax.broadcasted_iota(jnp.int32, spread.shape, 1)
-    ).astype(F32)
+    ).astype(F32).astype(BF16)
     loads[1].wait()
     hidden = jnp.where(ids_by_row(0) == lane_id, 0.0, HIDE)
     hidden = jnp.broadcast_to(hidden[:, None, :], (rows, group, hd)).reshape(flat, hd).astype(BF16)
@@ -145,15 +146,17 @@
         qs[h, :, 0:hd] = qv[:, h].astype(F32).reshape(flat, hd).astype(BF16)
         qs[h, :, hd:] = hidden
 
-    def prepare(d):
+    def prepare_keys(d):
         match = jnp.where(ids_by_row(d) == lane_id, 1.0, 0.0).astype(BF16)
         for h, key in enumerate(split_heads(ks.at[d])):
             kx[h, :, 0:hd] = key.astype(BF16)
             kx[h, :, hd:] = match
+
+    def prepare_values(d):
         for h, value in enumerate(split_heads(vs.at[d])):
             vt[h, 0:hd, :] = value.T.astype(BF16)
 
-    def attend(d, h):
+    def attend(d, h, part="all"):
         def extent(t):
             low, high = 0, rows
             if d == 0:
@@ -176,10 +179,20 @@
         def tile(t, top):
             low, high = extent(t)
             cols = slice(t * TILE, (t + 1) * TILE)
+            if part == "values":
+                p = later[h, :, cols]
+                new = jnp.dot(vt[h], p, preferred_element_type=F32)
+                acc[h, :, cols] = new + acc[h, :, cols] * shrink[h, 0:1, cols]
+                return
             if d > 0:
                 old = mstat[h, 0:1, cols]
                 top = jnp.maximum(old, top)
             p = jnp.exp2((held[t % 4, low:high, :] - top) * factor).astype(BF16)
+            if part == "keys":
+                later[h, :, cols] = p
+                shrink[h, :, cols] = jnp.broadcast_to(jnp.exp2((old - top) * factor), (8, TILE))
+                mstat[h, :, cols] = jnp.broadcast_to(top, (8, TILE))
+                return
             first, last = low // 128 * 128, -(-high // 128) * 128
             parts = [p]
             if low > first:
@@ -194,16 +207,20 @@
             mstat[h, :, cols] = jnp.broadcast_to(top, (8, TILE))
 
         tiles = flat // TILE
+        if part == "values":
+            for t in range(tiles):
+                tile(t, None)
+            return
         ready = [scores(t) for t in range(min(3, tiles))]
         for t in range(tiles):
             if t + 3 < tiles:
                 ready.append(scores(t + 3))
             tile(t, ready[t])
 
-    def wait_rest(d):
+    def wait_rest(d, some):
         if d % 2 == 0 and d // 2 < half:
             return
-        for j in range(chunks):
+        for j in some:
             if d % 2 == 0:
                 @pl.when(is_odd == 0)
                 def _():
@@ -222,7 +239,8 @@
     points = at_each_forward(1)
     loads[2].wait()
     loads[3].wait()
-    prepare(0)
+    prepare_keys(0)
+    prepare_values(0)
     for h in range(heads):
         attend(0, h)
         next(points, None)
@@ -231,10 +249,24 @@
     for k in range(1, half + 1):
         points = at_each_forward(k + 1)
         for d in (2 * k, 2 * k - 1):
+            if d == 2 * half - 1:
+                @pl.when(c >= d)
+                def _():
+                    wait_rest(d, range(1 + PARTS))
+                    prepare_keys(d)
+                    for h in range(heads):
+                        attend(d, h, "keys")
+                    wait_rest(d, range(1 + PARTS, chunks))
+                    prepare_values(d)
+                    for h in range(heads):
+                        attend(d, h, "values")
+                continue
+
             @pl.when(c >= d)
             def _():
-                wait_rest(d)
-                prepare(d)
+                wait_rest(d, range(chunks))
+                prepare_keys(d)
+                prepare_values(d)
 
             for h in range(heads):
                 @pl.when(c >= d)
@@ -244,32 +276,53 @@
         for _ in points:
             pass
 
-    def finish(i, carry):
-        start = pl.multiple_of(i * TILE, TILE)
-        cols = pl.ds(start, TILE)
+    def sub_id(width):
+        return lax.broadcasted_iota(jnp.int32, (8, width), 0)
+
+    pieces = flat // spread_rows
+    lines = []
+    for t in range(flat // TILE):
+        cols = slice(t * TILE, (t + 1) * TILE)
         line = jnp.zeros((1, TILE), F32)
         for h in range(heads):
-            got = acc[h, 0:hd, cols] * (1.0 / acc[h, hd:hd + 1, cols])
-            got = got.astype(BF16).astype(F32)
-            line = line + jnp.sum(got * swt[h], axis=0, keepdims=True)
-            out_ref[pl.ds(i * tile_pos, tile_pos), h] = got.T.reshape(tile_pos, group, hd).astype(BF16)
-        prow[:, cols] = jnp.broadcast_to(line, (8, TILE))
-        return carry
-
-    lax.fori_loop(0, flat // TILE, finish, 0)
-    for at in range(flat // spread_rows):
-        part[:, at * 128:(at + 1) * 128] = jnp.dot(
-            prow[:, at * spread_rows:(at + 1) * spread_rows], spread[...],
-            precision=lax.Precision.HIGHEST, preferred_element_type=F32)
+            got = (acc[h, 0:hd, cols] * (1.0 / acc[h, hd:hd + 1, cols])).astype(BF16)
+            done[h, :, cols] = got
+            line = line + jnp.sum(got.astype(F32) * swt[h], axis=0, keepdims=True)
+        lines.append(line)
+    for p in range(pieces):
+        span = spread_rows // TILE
+        line = jnp.concatenate(lines[p * span:(p + 1) * span], axis=1)
+        high = line.astype(BF16).astype(F32)
+        middle = (line - high).astype(BF16).astype(F32)
+        low = line - high - middle
+        three = jnp.where(sub_id(spread_rows) == 0, high, jnp.where(sub_id(spread_rows) == 1, middle, jnp.where(sub_id(spread_rows) == 2, low, 0.0)))
+        got = jnp.dot(three.astype(BF16), spread[...], preferred_element_type=F32)
+        part[:, p * 128:(p + 1) * 128] = jnp.sum(got, axis=0, keepdims=True)
     share = pltpu.make_async_remote_copy(
         src_ref=part, dst_ref=part_in, send_sem=score_sem.at[0], recv_sem=score_sem.at[1],
         device_id={"head": 1 - hc}, device_id_type=MESH)
     share.start()
+    for t in range(flat // TILE):
+        for h in range(heads):
+            got = done[h, :, t * TILE:(t + 1) * TILE].astype(F32).T
+            out_ref[t * tile_pos:(t + 1) * tile_pos, h] = got.reshape(tile_pos, group, hd).astype(BF16)
     for k in range(half + 1):
         for j in range(chunks):
             sends(k, j, lambda copy: copy.wait_send())
     share.wait()
-    score_ref[...] = (part[...] + part_in[...])[0:1, :]
+    score_ref[...] = part[...] + part_in[...]
+
+
+def put_out(attended_ref, score_ref, attended_out, score_out, sem):
+    rows = attended_ref.shape[0] // OUTS
+    copies = [pltpu.make_async_copy(score_ref, score_out, sem.at[OUTS])]
+    for i in range(OUTS):
+        span = pl.ds(i * rows, rows)
+        copies.append(pltpu.make_async_copy(attended_ref.at[span], attended_out.at[span], sem.at[i]))
+    for copy in copies:
+        copy.start()
+    for copy in copies:
+        copy.wait()
 
 
 def local(n, queries, keys, values, segments, score_weight):
@@ -283,7 +336,7 @@
         functools.partial(kernel, n, window),
         out_shape=(
             pltpu.VMEM(queries.shape, BF16),
-            jax.ShapeDtypeStruct((1, rows), F32),
+            pltpu.VMEM((1, rows), F32),
         ),
         in_specs=[anywhere] * 5,
         out_specs=(vmem, vmem),
@@ -301,10 +354,12 @@
             pltpu.VMEM((heads, 8, flat), F32),
             pltpu.VMEM((heads, hd + PAD, rows), BF16),
             pltpu.VMEM((heads, hd, TILE), F32),
-            pltpu.VMEM((128 * group, 128), F32),
-            pltpu.VMEM((8, flat), F32),
-            pltpu.VMEM((8, rows), F32),
-            pltpu.VMEM((8, rows), F32),
+            pltpu.VMEM((128 * group, 128), BF16),
+            pltpu.VMEM((heads, rows, flat), BF16),
+            pltpu.VMEM((heads, 8, flat), F32),
+            pltpu.VMEM((heads, hd, flat), BF16),
+            pltpu.VMEM((1, rows), F32),
+            pltpu.VMEM((1, rows), F32),
             pltpu.SemaphoreType.DMA((5,)),
             pltpu.SemaphoreType.DMA((window // 2, chunks)),
             pltpu.SemaphoreType.DMA((window // 2 + 1, chunks)),
@@ -313,6 +368,13 @@
         ],
         compiler_params=pltpu.CompilerParams(collective_id=0, has_side_effects=True),
     )(queries, keys.reshape(rows * heads, hd), values.reshape(rows * heads, hd), segments.reshape(1, rows), score_weight)
+    attended, score = pl.pallas_call(
+        put_out,
+        out_shape=(jax.ShapeDtypeStruct(attended.shape, BF16), jax.ShapeDtypeStruct(score.shape, F32)),
+        in_specs=[vmem] * 2,
+        out_specs=(anywhere, anywhere),
+        scratch_shapes=[pltpu.SemaphoreType.DMA((OUTS + 1,))],
+    )(pltpu.with_memory_space_constraint(attended, pltpu.VMEM), pltpu.with_memory_space_constraint(score, pltpu.VMEM))
     return attended, score.reshape(rows)
 
 

time: 26.3 us -> 23.1 us (0.88)
  local copies, waits for them, and re-layouts: 2.19 us -> 0 us
  Pallas kernels: 23.3 us -> 22.3 us
    unnamed x4 -> x0, local copies, waits for them, and re-layouts: 2.19 us -> none
    pallas_call x1, Pallas kernels: 23.3 us -> 21.3 us  [local(): pl.pallas_call(functools.partial(kernel, n, window), out_shape=(pltpu.VME...]
    pallas_call x0 -> x1, Pallas kernels: none -> 1.01 us  [local(): pl.pallas_call(put_out, out_shape=(jax.ShapeDtypeStruct(attended.shape, B...]
where the time goes in v2:
time: 23.1 us; the launch traced here: 22.9 us
  Pallas kernels  22.3 us (97%)
  between operations  0.64 us (3%)
    pallas_call x1, Pallas kernels, local(): pl.pallas_call(functools.partial(kernel, n, window), out_shape=(pltpu.VME...  21.3 us
    pallas_call x1, Pallas kernels, local(): pl.pallas_call(put_out, out_shape=(jax.ShapeDtypeStruct(attended.shape, B...  1.01 us

profile of v2, /device:TPU:17, one launch (start us, length us, event | category | flops | bytes accessed | tf_op | source)
XLA Modules:
  0.0 22.9 jit_solution(10054677417279063787)
XLA Ops:
  0.6 21.3 %shard_map.68 = (bf16[256,2,8,128]{3,2,1,0:T(8,128)(2,1)S(1)}, f32[1,256]{1,0:T(1,128)S(1)}) custom-call(bf16[256,2,8,128]{3,2,1,0:T(8,128)(2,1)} %q_hbm.1, bf16[512,128]{1,0:T(8,128)(2,1)} %bitcast.4, bf16[512,128]{1,0:T(8,128)(2,1)} %bitcast.5, s32[1,256]{1,0:T(1,128)} %bitcast.6, bf16[2,8,128]{2,1,0:T(8,128)(2,1)} %sw_hbm.1), custom_call_target="tpu_custom_call" | custom-call | tf_op jit(solution)/shard_map/pallas_call | solution.py:335
  21.9 1.0 %shard_map.69 = (bf16[256,2,8,128]{3,2,1,0:T(8,128)(2,1)}, f32[1,256]{1,0:T(1,128)}) custom-call(bf16[256,2,8,128]{3,2,1,0:T(8,128)(2,1)S(1)} %get-tuple-element.6.attended_ref, f32[1,256]{1,0:T(1,128)S(1)} %get-tuple-element.7.score_ref), custom_call_target="tpu_custom_call" | custom-call | tf_op jit(solution)/shard_map/pallas_call | solution.py:371

commit v3 on v2

--- a/solution.py
+++ b/solution.py
@@ -16,11 +16,12 @@
 HIDE = -1e30
 PARTS = 2
 OUTS = 4
+DETOUR = 1
 
 
 def kernel(n, window, q_hbm, k_hbm, v_hbm, ids_hbm, sw_hbm, out_ref, score_ref,
            ks, vs, ids, qv, swv, wide, qs, kx, held, acc, mstat, vt, swt, spread, later, shrink, done, part, part_in,
-           load_sem, lane_send, cross_send, recv, score_sem):
+           load_sem, lane_send, cross_send, detour_send, recv, score_sem):
     rows, heads, group, hd = q_hbm.shape
     flat = rows * group
     half = window // 2
@@ -33,6 +34,7 @@
     tile_pos = TILE // group
     cut = rows * heads // PARTS
     chunks = 1 + 2 * PARTS
+    detour = range(chunks - DETOUR, chunks) if half >= 2 else range(0)
 
     barrier = pltpu.get_barrier_semaphore()
     has_next = c + 2 < n
@@ -84,6 +86,16 @@
             send_sem=cross_send.at[k, j], recv_sem=recv.at[2 * k - 2, j],
             device_id={"ctx": partner}, device_id_type=MESH)
 
+    def detours(act):
+        d = 2 * half - 3
+        for i, j in enumerate(detour):
+            @pl.when((c >= d) & has_next & (is_odd == 0))
+            def _():
+                act(j, pltpu.make_async_remote_copy(
+                    src_ref=piece(d, j, False), dst_ref=piece(d + 2, j, False),
+                    send_sem=detour_send.at[i], recv_sem=recv.at[d + 1, j],
+                    device_id={"ctx": c + 2}, device_id_type=MESH))
+
     def sends(k, j, act):
         held_here = c >= 2 * k
         if k < half:
@@ -94,7 +106,7 @@
             @pl.when(held_here & (is_odd == 0))
             def _():
                 act(cross_even(k, j))
-        if k >= 1:
+        if k >= 1 and not (k == half and j in detour):
             @pl.when(held_here & (is_odd == 1))
             def _():
                 act(cross_odd(k, j))
@@ -179,27 +191,26 @@
         def tile(t, top):
             low, high = extent(t)
             cols = slice(t * TILE, (t + 1) * TILE)
+            first, last = low // 128 * 128, -(-high // 128) * 128
             if part == "values":
-                p = later[h, :, cols]
-                new = jnp.dot(vt[h], p, preferred_element_type=F32)
+                new = jnp.dot(vt[h, :, first:last], later[h, first:last, cols], preferred_element_type=F32)
                 acc[h, :, cols] = new + acc[h, :, cols] * shrink[h, 0:1, cols]
                 return
             if d > 0:
                 old = mstat[h, 0:1, cols]
                 top = jnp.maximum(old, top)
             p = jnp.exp2((held[t % 4, low:high, :] - top) * factor).astype(BF16)
-            if part == "keys":
-                later[h, :, cols] = p
-                shrink[h, :, cols] = jnp.broadcast_to(jnp.exp2((old - top) * factor), (8, TILE))
-                mstat[h, :, cols] = jnp.broadcast_to(top, (8, TILE))
-                return
-            first, last = low // 128 * 128, -(-high // 128) * 128
             parts = [p]
             if low > first:
                 parts = [jnp.zeros((low - first, TILE), BF16)] + parts
             if last > high:
                 parts = parts + [jnp.zeros((last - high, TILE), BF16)]
             p = jnp.concatenate(parts, axis=0) if len(parts) > 1 else p
+            if part == "keys":
+                later[h, first:last, cols] = p
+                shrink[h, :, cols] = jnp.broadcast_to(jnp.exp2((old - top) * factor), (8, TILE))
+                mstat[h, :, cols] = jnp.broadcast_to(top, (8, TILE))
+                return
             new = jnp.dot(vt[h, :, first:last], p, preferred_element_type=F32)
             if d > 0:
                 new = new + acc[h, :, cols] * jnp.exp2((old - top) * factor)
@@ -228,53 +239,55 @@
             else:
                 wait_piece(d, j)
 
-    def at_each_forward(k):
-        plan = [[0, 1]] + [[j] for j in range(2, chunks)]
-        for some in plan:
-            if k <= half:
-                for j in some:
-                    forward(k, j)
-            yield
-
-    points = at_each_forward(1)
+    def when_held(d, act, *args):
+        @pl.when(c >= d)
+        def _():
+            act(*args)
+
+    def forwards(k, some):
+        if k <= half:
+            for j in some:
+                forward(k, j)
+
+    def take_keys(d):
+        wait_rest(d, range(1 + PARTS))
+        prepare_keys(d)
+
+    def take_values(d):
+        wait_rest(d, range(1 + PARTS, chunks))
+        if d == 2 * half - 3:
+            detours(lambda j, copy: copy.start())
+        prepare_values(d)
+
     loads[2].wait()
     loads[3].wait()
     prepare_keys(0)
     prepare_values(0)
-    for h in range(heads):
+    attend(0, 0)
+    forwards(1, range(2))
+    for h in range(1, heads):
         attend(0, h)
-        next(points, None)
-    for _ in points:
-        pass
+    ahead = 2
     for k in range(1, half + 1):
-        points = at_each_forward(k + 1)
-        for d in (2 * k, 2 * k - 1):
-            if d == 2 * half - 1:
-                @pl.when(c >= d)
-                def _():
-                    wait_rest(d, range(1 + PARTS))
-                    prepare_keys(d)
-                    for h in range(heads):
-                        attend(d, h, "keys")
-                    wait_rest(d, range(1 + PARTS, chunks))
-                    prepare_values(d)
-                    for h in range(heads):
-                        attend(d, h, "values")
-                continue
-
-            @pl.when(c >= d)
-            def _():
-                wait_rest(d, range(chunks))
-                prepare_keys(d)
-                prepare_values(d)
-
-            for h in range(heads):
-                @pl.when(c >= d)
-                def _():
-                    attend(d, h)
-                next(points, None)
-        for _ in points:
-            pass
+        forwards(k, range(ahead, 1 + PARTS))
+        due = [range(1 + PARTS, 1 + PARTS + PARTS // 2), range(1 + PARTS + PARTS // 2, chunks)]
+        when_held(2 * k, take_keys, 2 * k)
+        for h in range(heads):
+            when_held(2 * k, attend, 2 * k, h, "keys")
+            if h < 2:
+                forwards(k, due[h])
+        when_held(2 * k, take_values, 2 * k)
+        for h in range(heads):
+            when_held(2 * k, attend, 2 * k, h, "values")
+        d = 2 * k - 1
+        when_held(d, take_keys, d)
+        for h in range(heads):
+            when_held(d, attend, d, h, "keys")
+            if h == 0:
+                forwards(k + 1, range(ahead))
+        when_held(d, take_values, d)
+        for h in range(heads):
+            when_held(d, attend, d, h, "values")
 
     def sub_id(width):
         return lax.broadcasted_iota(jnp.int32, (8, width), 0)
@@ -309,6 +322,7 @@
     for k in range(half + 1):
         for j in range(chunks):
             sends(k, j, lambda copy: copy.wait_send())
+    detours(lambda j, copy: copy.wait_send())
     share.wait()
     score_ref[...] = part[...] + part_in[...]
 
@@ -363,6 +377,7 @@
             pltpu.SemaphoreType.DMA((5,)),
             pltpu.SemaphoreType.DMA((window // 2, chunks)),
             pltpu.SemaphoreType.DMA((window // 2 + 1, chunks)),
+            pltpu.SemaphoreType.DMA((max(1, DETOUR),)),
             pltpu.SemaphoreType.DMA((window, chunks)),
             pltpu.SemaphoreType.DMA((2,)),
         ],

time: 23.1 us -> 22.2 us (0.961)
  Pallas kernels: 22.3 us -> 21.4 us
    pallas_call x1, Pallas kernels: 21.3 us -> 20.4 us  [local(): pl.pallas_call(functools.partial(kernel, n, window), out_shape=(pltpu.VME...]
where the time goes in v3:
time: 22.2 us; the launch traced here: 22 us
  Pallas kernels  21.4 us (96%)
  between operations  0.64 us (3%)
    pallas_call x1, Pallas kernels, local(): pl.pallas_call(functools.partial(kernel, n, window), out_shape=(pltpu.VME...  20.4 us
    pallas_call x1, Pallas kernels, local(): pl.pallas_call(put_out, out_shape=(jax.ShapeDtypeStruct(attended.shape, B...  1.01 us

profile of v3, /device:TPU:17, one launch (start us, length us, event | category | flops | bytes accessed | tf_op | source)
XLA Modules:
  0.0 22.0 jit_solution(15453781961672560919)
XLA Ops:
  0.6 20.4 %shard_map.68 = (bf16[256,2,8,128]{3,2,1,0:T(8,128)(2,1)S(1)}, f32[1,256]{1,0:T(1,128)S(1)}) custom-call(bf16[256,2,8,128]{3,2,1,0:T(8,128)(2,1)} %q_hbm.1, bf16[512,128]{1,0:T(8,128)(2,1)} %bitcast.4, bf16[512,128]{1,0:T(8,128)(2,1)} %bitcast.5, s32[1,256]{1,0:T(1,128)} %bitcast.6, bf16[2,8,128]{2,1,0:T(8,128)(2,1)} %sw_hbm.1), custom_call_target="tpu_custom_call" | custom-call | tf_op jit(solution)/shard_map/pallas_call | solution.py:349
  21.0 1.0 %shard_map.69 = (bf16[256,2,8,128]{3,2,1,0:T(8,128)(2,1)}, f32[1,256]{1,0:T(1,128)}) custom-call(bf16[256,2,8,128]{3,2,1,0:T(8,128)(2,1)S(1)} %get-tuple-element.6.attended_ref, f32[1,256]{1,0:T(1,128)S(1)} %get-tuple-element.7.score_ref), custom_call_target="tpu_custom_call" | custom-call | tf_op jit(solution)/shard_map/pallas_call | solution.py:386
